TPU v7x, 256 devices: a whole 4x4x8 slice. The times are simulated.
256 devices in a mesh: row: 8 (over z_hi, core), col: 32 (over y, z_lo, x).
Axes of the slice: x: 4, y: 4, z: 8 (z_hi: 4, z_lo: 2; z = z_hi * 2 + z_lo), core: 2. Of those that a mesh axis runs over, the one named last changes fastest.
Arguments:
- features: bfloat16 [65536, 512], P('col'), may hold values from -6 to 6
- weight_raw: bfloat16 [512, 512], P('col'), may hold values from -0.0234375 to 0.0234375
- direction_raw: bfloat16 [512, 512], P('col'), may hold values from -0.0014648438 to 0.0014648438
- panel_index: int32 [4096], P('row'), may hold values from 0 to 65535, as said below
- labels: int32 [4096, 65536], P('row', 'col'), may hold values 0 or 1
Outputs:
- gradient: float32 [512, 512], P('col')
- hess_vec: float32 [512, 512], P('col')
Inputs may be any that keep to these rules, and one draw needn't show every extreme that they name: `panel_index`: distinct compounds; the largest entry is 65535.
All inputs are finite; a program needn't handle non-finite values. No bound on the sum of `labels` on one device may be relied on, other than what follows from the above.
Results may differ from a plain program's by a relative error of at most 0.0033.
Values may be sent and summed in bfloat16 or wider, within the bound.
No kernel may reach another device: no remote copies, remote signals or barrier semaphores. Data moves between devices by JAX's collectives and lax.ppermute only.
A program may use at most 64 MiB of HBM per device.

v0:
```python
import functools
import math

import jax
import jax.numpy as jnp
from jax import lax
from jax.experimental import pallas as pl
from jax.experimental.pallas import tpu as pltpu
from jax.sharding import PartitionSpec as P

BF16, F32, I32 = jnp.bfloat16, jnp.float32, jnp.int32
ROUND_ROWS = 32
STEP_COLUMNS = 512
LOADS = 4

in_vmem = functools.partial(pl.BlockSpec, memory_space=pltpu.VMEM)
in_smem = functools.partial(pl.BlockSpec, memory_space=pltpu.SMEM)
in_place = functools.partial(pl.BlockSpec, memory_space=pl.ANY)


def params(mebibytes=8):
    return pltpu.CompilerParams(vmem_limit_bytes=mebibytes << 20)


def rows_of(a, b):
    return jnp.dot(a, b, preferred_element_type=F32)


def exchange(value, mask):
    return lax.ppermute(value, "row", [(i, i ^ mask) for i in range(lax.axis_size("row"))])


def ranks(panel_row, bits):
    count = panel_row.shape[1]
    owner_row = lax.shift_right_logical(panel_row, bits)
    owner = jnp.broadcast_to(owner_row, (128, count)).T[:, :1]
    same = owner == owner_row
    down, along = (lax.broadcasted_iota(I32, (count, count), axis) for axis in (0, 1))
    rank_row = jnp.sum(jnp.where(same & (down < along), 1, 0), axis=0, keepdims=True)
    rank = jnp.sum(jnp.where(same & (along < down), 1, 0), axis=1, keepdims=True)
    return owner_row, rank_row, owner, rank


def own_places(panel_row, owner_row, rank_row, col_count, step):
    count = panel_row.shape[1]
    me = lax.axis_index("col")
    slot = jnp.where(owner_row == me, rank_row - step * ROUND_ROWS, -1)
    mine = slot == lax.broadcasted_iota(I32, (ROUND_ROWS, count), 0)
    return jnp.sum(jnp.where(mine, panel_row + (1 - me * col_count), 0), axis=1, keepdims=True) - 1


def load_columns(features, panel_row):
    col_count, dim = features.shape
    count = panel_row.shape[1]
    bits = col_count.bit_length() - 1
    chunk = col_count // LOADS
    assert col_count == 1 << bits

    def body(row_from, features_hbm, table, rounds, places, blank, row_ref, zeros, arrived):
        row_load = pltpu.make_async_copy(row_from, row_ref, arrived.at[LOADS + 1])
        row_load.start()
        loads = []
        for i in range(LOADS):
            part = pl.ds(i * chunk, chunk)
            loads.append(pltpu.make_async_copy(features_hbm.at[part], table.at[part], arrived.at[i]))
            loads[i].start()
        zeros[...] = jnp.zeros_like(zeros)
        loads.append(pltpu.make_async_copy(zeros, blank, arrived.at[LOADS]))
        loads[LOADS].start()
        row_load.wait()
        row = row_ref[...]
        owner_row, rank_row, _, _ = ranks(row, bits)
        rounds[0] = jnp.max(rank_row) // ROUND_ROWS + 1
        places[...] = jnp.broadcast_to(own_places(row, owner_row, rank_row, col_count, 0), (ROUND_ROWS, 128))
        for load in loads:
            load.wait()

    return pl.pallas_call(
        body,
        name="load_columns",
        out_shape=(
            jax.ShapeDtypeStruct(features.shape, BF16),
            jax.ShapeDtypeStruct((1,), I32),
            jax.ShapeDtypeStruct((ROUND_ROWS, 128), I32),
            jax.ShapeDtypeStruct((count, dim), BF16),
        ),
        in_specs=[in_place(), in_place()],
        out_specs=(in_vmem(), in_smem(), in_vmem(), in_place()),
        scratch_shapes=[
            pltpu.VMEM((1, count), I32),
            pltpu.VMEM((count, dim), BF16),
            pltpu.SemaphoreType.DMA((LOADS + 2,)),
        ],
        compiler_params=params(),
    )(panel_row, features)


def pack_rows(columns, panel_row, extra_rows, places, step):
    n_col = lax.axis_size("col")
    n_slots = n_col * ROUND_ROWS
    col_count, dim = columns.shape
    count = panel_row.shape[1]
    n_extra = extra_rows[0].shape[0] if extra_rows else 0
    bits = col_count.bit_length() - 1

    def body(step_ref, row_ref, columns_ref, places_ref, *refs):
        extra, (out, pick_out, tail, arrived) = refs[:-4], refs[-4:]
        for core, source in enumerate(extra):
            @pl.when(lax.axis_index("row") % 2 == core)
            def _():
                pltpu.make_async_copy(source, tail, arrived).start()
        row, step = row_ref[...], step_ref[0]
        owner_row, rank_row, owner, rank = ranks(row, bits)
        wanted = places_ref[:, :1] if extra else own_places(row, owner_row, rank_row, col_count, step)
        chosen = (wanted == lax.broadcasted_iota(I32, (ROUND_ROWS, col_count), 1)).astype(F32).astype(BF16)
        message = rows_of(chosen, columns_ref[...]).astype(BF16)
        rank = rank - step * ROUND_ROWS
        slot = jnp.where((rank >= 0) & (rank < ROUND_ROWS), owner * ROUND_ROWS + rank, -1)
        pick = slot == lax.broadcasted_iota(I32, (count, n_slots), 1)
        pick_out[...] = pick.astype(F32).astype(BF16)
        if extra:
            pltpu.make_async_copy(extra[0], tail, arrived).wait()
            message = jnp.concatenate([message, tail[...]], axis=0)
        for peer in range(n_col):
            out[peer] = message

    return pl.pallas_call(
        body,
        name="pack_rows",
        out_shape=(
            jax.ShapeDtypeStruct((n_col, ROUND_ROWS + n_extra, dim), BF16),
            jax.ShapeDtypeStruct((count, n_slots), BF16),
        ),
        in_specs=[in_smem(), in_vmem(), in_vmem(), in_vmem()] + [in_place()] * len(extra_rows),
        out_specs=(in_vmem(), in_vmem()),
        scratch_shapes=[pltpu.VMEM((max(n_extra, 16), dim), BF16), pltpu.SemaphoreType.DMA(())],
        compiler_params=params(),
    )(step, panel_row, columns, places, *extra_rows)


def panel_part(received):
    n_col, _, dim = received.shape
    return received[:, :ROUND_ROWS, :].reshape(n_col * ROUND_ROWS, dim)


def add_round(pick, received, panel):
    def body(pick_ref, received_ref, panel_ref, out):
        rows = rows_of(pick_ref[...], panel_part(received_ref[...]))
        out[...] = (panel_ref[...].astype(F32) + rows).astype(BF16)

    return pl.pallas_call(
        body,
        name="add_round",
        out_shape=jax.ShapeDtypeStruct(panel.shape, BF16),
        in_specs=[in_vmem(), in_vmem(), in_vmem()],
        out_specs=in_vmem(),
        compiler_params=params(),
    )(pick, received, panel)


def symmetric_matrix(received):
    dim = received.shape[2]

    def body(received_ref, out):
        raw = received_ref[:, ROUND_ROWS:, :].reshape(dim, dim).astype(F32)
        out[...] = ((raw + raw.T) * 0.5).astype(BF16)

    return pl.pallas_call(
        body,
        name="symmetric_matrix",
        out_shape=jax.ShapeDtypeStruct((dim, dim), BF16),
        in_specs=[in_vmem()],
        out_specs=in_vmem(),
        compiler_params=params(),
    )(received)


def pairs_of(rows, matrix, columns):
    projected = rows_of(rows, matrix).astype(BF16)
    return lax.dot_general(projected, columns, (((1,), (1,)), ((), ())), preferred_element_type=F32)


def panel_product(turned, weights, columns):
    half = rows_of(turned, rows_of(weights, columns).astype(BF16))
    return half + half.T


def own_pairs(pick, received, later, kept_matrix, columns, labels):
    count, dim = later.shape

    def body(pick_ref, received_ref, later_ref, matrix_ref, columns_ref, labels_hbm, panel, turned, pairs, labels_out, arrived):
        load = pltpu.make_async_copy(labels_hbm, labels_out, arrived)
        load.start()
        rows = rows_of(pick_ref[...], panel_part(received_ref[...]))
        panel[...] = (rows + later_ref[...].astype(F32)).astype(BF16)
        pairs[...] = pairs_of(panel[...], matrix_ref[...], columns_ref[...])
        turned[...] = panel[...].T
        load.wait()

    return pl.pallas_call(
        body,
        name="own_pairs",
        out_shape=(
            jax.ShapeDtypeStruct((count, dim), BF16),
            jax.ShapeDtypeStruct((dim, count), BF16),
            jax.ShapeDtypeStruct((count, columns.shape[0]), F32),
            jax.ShapeDtypeStruct(labels.shape, I32),
        ),
        in_specs=[in_vmem()] * 5 + [in_place()],
        out_specs=(in_vmem(),) * 4,
        scratch_shapes=[pltpu.SemaphoreType.DMA(())],
        compiler_params=params(),
    )(pick, received, later, kept_matrix, columns, labels)


def given_part(panel, turned, other_matrix, own, columns, labels):
    count, dim = panel.shape
    col_count = columns.shape[0]

    def body(panel_ref, turned_ref, matrix_ref, own_ref, columns_ref, labels_ref, given, kept_weights, weights):
        first = lax.axis_index("row") % 2 == 0
        projected = rows_of(panel_ref[...], matrix_ref[...]).astype(BF16)
        for start in range(0, col_count, STEP_COLUMNS):
            part = pl.ds(start, STEP_COLUMNS)
            other = lax.dot_general(
                projected, columns_ref[part], (((1,), (1,)), ((), ())), preferred_element_type=F32
            )
            mine = own_ref[:, part]
            margin = jnp.where(first, mine, other)
            change = jnp.where(first, other, mine)
            probability = 1.0 / (1.0 + jnp.exp(-margin))
            residual = probability - labels_ref[:, part].astype(F32)
            curvature = probability * (1.0 - probability) * change
            kept_weights[:, part] = jnp.where(first, residual, curvature).astype(BF16)
            weights[:, part] = jnp.where(first, curvature, residual).astype(BF16)
        given[...] = panel_product(turned_ref[...], weights[...], columns_ref[...]).astype(BF16)

    return pl.pallas_call(
        body,
        name="given_part",
        out_shape=(jax.ShapeDtypeStruct((dim, dim), BF16), jax.ShapeDtypeStruct((count, col_count), BF16)),
        in_specs=[in_vmem()] * 6,
        out_specs=(in_vmem(), in_vmem()),
        scratch_shapes=[pltpu.VMEM((count, col_count), BF16)],
        compiler_params=params(16),
    )(panel, turned, other_matrix, own, columns, labels)


def kept_part(turned, weights, columns):
    dim = columns.shape[1]

    def body(turned_ref, weights_ref, columns_ref, out):
        out[...] = panel_product(turned_ref[...], weights_ref[...], columns_ref[...])

    return pl.pallas_call(
        body,
        name="kept_part",
        out_shape=jax.ShapeDtypeStruct((dim, dim), F32),
        in_specs=[in_vmem()] * 3,
        out_specs=in_vmem(),
        compiler_params=params(),
    )(turned, weights, columns)


def shards(features, weight_raw, direction_raw, panel_index, labels):
    n_row, n_col = lax.axis_size("row"), lax.axis_size("col")
    col_count, dim = features.shape
    count = panel_index.shape[0]
    features, weight_raw, direction_raw, labels = (
        pltpu.with_memory_space_constraint(x, pltpu.HBM) for x in (features, weight_raw, direction_raw, labels)
    )
    panel_row = panel_index.reshape(1, count)
    first = jnp.zeros((1,), I32)
    columns, rounds, places, blank = load_columns(features, panel_row)

    def another(state):
        step, rows = state
        message, pick = pack_rows(columns, panel_row, (), places, step)
        return step + 1, add_round(pick, lax.all_to_all(message, "col", 0, 0, tiled=True), rows)

    _, later = lax.while_loop(lambda state: state[0][0] < rounds[0], another, (first + 1, blank))
    panel_row, later = lax.optimization_barrier((panel_row, later))
    columns = pltpu.with_memory_space_constraint(columns, pltpu.VMEM)
    sent, pick = pack_rows(columns, panel_row, (weight_raw, direction_raw), places, first)
    received = lax.all_to_all(sent, "col", 0, 0, tiled=True)
    kept_matrix = symmetric_matrix(received)
    other_matrix = exchange(kept_matrix, 1)
    panel, turned, own, labels = own_pairs(pick, received, later, kept_matrix, columns, labels)
    given, weights = given_part(panel, turned, other_matrix, own, columns, labels)
    swapped = exchange(given, 1)
    kept = kept_part(turned, weights, columns)
    chip_sum = (kept + swapped.astype(F32)).astype(BF16)
    parts = lax.all_to_all(chip_sum.reshape(n_col, dim // n_col, dim), "col", 0, 0, tiled=True)
    mine = jnp.sum(parts.astype(F32), axis=0)
    near = mine + exchange(mine, 2)
    scale = 0.5 / math.sqrt(count * n_row * col_count * n_col)
    total = (near + exchange(near, 6)) * scale
    other = exchange(total, 1)
    on_first = lax.axis_index("row") % 2 == 0
    return jnp.where(on_first, total, other), jnp.where(on_first, other, total)


def solution(mesh):
    return jax.shard_map(
        shards,
        mesh=mesh,
        in_specs=(P("col", None), P("col", None), P("col", None), P("row"), P("row", "col")),
        out_specs=(P("col", None), P("col", None)),
        check_vma=False,
    )
```

profile of v0, /device:TPU:1, one launch (start us, length us, event | category | flops | bytes accessed | tf_op | source)
XLA Modules:
  0.0 76.2 jit_solution(14140986861377805429)
XLA Ops:
  0.6 0.0 copy-start.5
  0.6 2.3 %load_columns.1 = (bf16[2048,512]{1,0:T(8,128)(2,1)S(1)}, s32[1]{0:T(128)}, s32[32,128]{1,0:T(8,128)S(1)}, bf16[512,512]{1,0:T(8,128)(2,1)}) custom-call(s32[1,512]{1,0:T(1,128)} %bitcast.5, bf16[2048,512]{1,0:T(8,128)(2,1)} %features_hbm.1), custom_call_target="tpu_custom_call" | custom-call | tf_op jit(solution)/shard_map/load_columns/pallas_call | solution.py:78
  2.9 0.0 copy-done.5
  3.0 0.7 while.10
  3.6 0.9 %pack_rows.2 = (bf16[32,48,512]{2,1,0:T(8,128)(2,1)S(1)}, bf16[512,1024]{1,0:T(8,128)(2,1)S(1)}) custom-call(s32[1]{0:T(128)} %constant.26.clone.1.step_ref, s32[1,512]{1,0:T(1,128)S(1)} %get-tuple-element.147, bf16[2048,512]{1,0:T(8,128)(2,1)S(1)} %get-tuple-element.135, s32[32,128]{1,0:T(8,128)S(1)} %get-tuple-element.142, bf16[16,512]{1,0:T(8,128)(2,1)} %refs_0_.1, ...), custom_call_target="tpu_custom_call" | custom-call | tf_op jit(solution)/shard_map/pack_rows/pallas_call | solution.py:127
  4.6 0.0 copy-start.4
  4.6 30.3 %all_to_all.15.received_ref = bf16[32,48,512]{2,1,0:T(8,128)(2,1)S(1)} all-to-all(bf16[32,48,512]{2,1,0:T(8,128)(2,1)S(1)} %get-tuple-element.58), channel_id=1, replica_groups=mesh['row'=8,'col'=32] {'col'}, dimensions={0} | all-to-all | bytes 3145728 | tf_op jit(solution)/shard_map/all_to_all | solution.py:285
  34.8 0.2 symmetric_matrix.1.matrix_ref
  35.1 2.7 %collective-permute-start = (bf16[512,512]{1,0:T(8,128)(2,1)S(1)}, bf16[512,512]{1,0:T(8,128)(2,1)S(1)}, u32[]{:S(2)}, u32[]{:S(2)}) collective-permute-start(bf16[512,512]{1,0:T(8,128)(2,1)S(1)} %symmetric_matrix.1.matrix_ref), channel_id=1, source_target_pairs={{0,32},{32,0},{64,96},{96,64},{128,160},{160,128},{192,224},{224,1... | collective-permute-start | bytes 1572872 | tf_op jit(solution)/shard_map/ppermute | solution.py:30
  37.8 0.0 copy-done.4
  37.8 2.2 %own_pairs.1 = (bf16[512,512]{1,0:T(8,128)(2,1)S(1)}, bf16[512,512]{1,0:T(8,128)(2,1)S(1)}, f32[512,2048]{1,0:T(8,128)S(1)}, s32[512,2048]{1,0:T(8,128)S(1)}) custom-call(bf16[512,1024]{1,0:T(8,128)(2,1)S(1)} %get-tuple-element.57.pick_ref, bf16[32,48,512]{2,1,0:T(8,128)(2,1)S(1)} %all_to_all.15.received_ref, bf16[512,512]{1,0:T(8,128)(2,1)S(1)} %copy-done.4, ...), custom_call_target="tpu_custom_call" | custom-call | tf_op jit(solution)/shard_map/own_pairs/pallas_call | solution.py:200
  40.0 0.0 collective-permute-done.matrix_ref
  40.0 3.9 %given_part.1 = (bf16[512,512]{1,0:T(8,128)(2,1)S(1)}, bf16[512,2048]{1,0:T(8,128)(2,1)S(1)}) custom-call(bf16[512,512]{1,0:T(8,128)(2,1)S(1)} %get-tuple-element.61.panel_ref, bf16[512,512]{1,0:T(8,128)(2,1)S(1)} %get-tuple-element.60.turned_ref, bf16[512,512]{1,0:T(8,128)(2,1)S(1)} %collective-permute-done.matrix_ref, ...), custom_call_target="tpu_custom_call" | custom-call | tf_op jit(solution)/shard_map/given_part/pallas_call | solution.py:238
  43.9 0.1 collective-permute-start.1
  44.0 1.8 %kept_part.1 = f32[512,512]{1,0:T(8,128)S(1)} custom-call(bf16[512,512]{1,0:T(8,128)(2,1)S(1)} %get-tuple-element.60.turned_ref, bf16[512,2048]{1,0:T(8,128)(2,1)S(1)} %get-tuple-element.64.weights_ref, bf16[2048,512]{1,0:T(8,128)(2,1)S(1)} %get-tuple-element.135), custom_call_target="tpu_custom_call" | custom-call | tf_op jit(solution)/shard_map/kept_part/pallas_call | solution.py:255
  45.8 0.1 collective-permute-done.1
  45.9 0.2 add_convert_fusion
  46.1 14.0 %all_to_all.16 = bf16[32,16,512]{2,1,0:T(8,128)(2,1)S(1)} all-to-all(bf16[32,16,512]{2,1,0:T(8,128)(2,1)S(1)} %bitcast.4), channel_id=1, replica_groups=mesh['row'=8,'col'=32] {'col'}, dimensions={0} | all-to-all | bytes 1048576 | tf_op jit(solution)/shard_map/all_to_all | solution.py:293
  60.1 0.1 convert_reduce_fusion
  60.2 3.1 %collective-permute-start.2 = (f32[16,512]{1,0:T(8,128)S(1)}, f32[16,512]{1,0:T(8,128)S(1)}, u32[]{:S(2)}, u32[]{:S(2)}) collective-permute-start(f32[16,512]{1,0:T(8,128)S(1)} %convert_reduce_fusion), channel_id=1, source_target_pairs={{0,64},{32,96},{64,0},{96,32},{128,192},{160,224},{192,128},{224,1... | collective-permute-start | bytes 98312 | tf_op jit(solution)/shard_map/ppermute | solution.py:30
  63.3 1.6 %collective-permute-done.2 = f32[16,512]{1,0:T(8,128)S(1)} collective-permute-done((f32[16,512]{1,0:T(8,128)S(1)}, f32[16,512]{1,0:T(8,128)S(1)}, u32[]{:S(2)}, u32[]{:S(2)}) %collective-permute-start.2) | collective-permute-done | bytes 32800 | tf_op jit(solution)/shard_map/ppermute | solution.py:30
  64.9 4.1 %collective-permute-start.3 = (f32[16,512]{1,0:T(8,128)S(1)}, f32[16,512]{1,0:T(8,128)S(1)}, u32[]{:S(2)}, u32[]{:S(2)}) collective-permute-start(f32[16,512]{1,0:T(8,128)S(1)} %add.18), channel_id=1, source_target_pairs={{0,192},{32,224},{64,128},{96,160},{128,64},{160,96},{192,0},{224,... | collective-permute-start | bytes 98312 | tf_op jit(solution)/shard_map/ppermute | solution.py:30
  69.1 1.3 %collective-permute-done.3 = f32[16,512]{1,0:T(8,128)S(1)} collective-permute-done((f32[16,512]{1,0:T(8,128)S(1)}, f32[16,512]{1,0:T(8,128)S(1)}, u32[]{:S(2)}, u32[]{:S(2)}) %collective-permute-start.3) | collective-permute-done | bytes 32800 | tf_op jit(solution)/shard_map/ppermute | solution.py:30
  70.4 4.3 %collective-permute-start.4 = (f32[16,512]{1,0:T(8,128)S(1)}, f32[16,512]{1,0:T(8,128)S(1)}, u32[]{:S(2)}, u32[]{:S(2)}) collective-permute-start(f32[16,512]{1,0:T(8,128)S(1)} %add_multiply_fusion), channel_id=1, source_target_pairs={{0,32},{32,0},{64,96},{96,64},{128,160},{160,128},{192,224},{224,1... | collective-permute-start | bytes 98312 | tf_op jit(solution)/shard_map/ppermute | solution.py:30
  74.7 0.9 %collective-permute-done.4 = f32[16,512]{1,0:T(8,128)S(1)} collective-permute-done((f32[16,512]{1,0:T(8,128)S(1)}, f32[16,512]{1,0:T(8,128)S(1)}, u32[]{:S(2)}, u32[]{:S(2)}) %collective-permute-start.4) | collective-permute-done | bytes 32800 | tf_op jit(solution)/shard_map/ppermute | solution.py:30
  75.6 0.6 broadcast_select_fusion
  (2 shorter events, 0.0 us)
Async XLA Ops:
  0.6 2.3 %copy-start.5 = (s32[512]{0:T(512)S(1)}, s32[512]{0:T(512)}, u32[]{:S(2)}) copy-start(s32[512]{0:T(512)} %param.10) | copy-start | bytes 6148
  4.6 33.2 %copy-start.4 = (bf16[512,512]{1,0:T(8,128)(2,1)S(1)}, bf16[512,512]{1,0:T(8,128)(2,1)}, u32[]{:S(2)}) copy-start(bf16[512,512]{1,0:T(8,128)(2,1)} %get-tuple-element.59.later_ref) | copy-start | bytes 1572868
  35.1 4.9 %collective-permute-start = (bf16[512,512]{1,0:T(8,128)(2,1)S(1)}, bf16[512,512]{1,0:T(8,128)(2,1)S(1)}, u32[]{:S(2)}, u32[]{:S(2)}) collective-permute-start(bf16[512,512]{1,0:T(8,128)(2,1)S(1)} %symmetric_matrix.1.matrix_ref), channel_id=1, source_target_pairs={{0,32},{32,0},{64,96},{96,64},{128,160},{160,128},{192,224},{224,1... | collective-permute-start | bytes 1572872 | tf_op jit(solution)/shard_map/ppermute | solution.py:30
  43.9 2.0 %collective-permute-start.1 = (bf16[512,512]{1,0:T(8,128)(2,1)S(1)}, bf16[512,512]{1,0:T(8,128)(2,1)S(1)}, u32[]{:S(2)}, u32[]{:S(2)}) collective-permute-start(bf16[512,512]{1,0:T(8,128)(2,1)S(1)} %get-tuple-element.65), channel_id=1, source_target_pairs={{0,32},{32,0},{64,96},{96,64},{128,160},{160,128},{192,224},{224,1... | collective-permute-start | bytes 1572872 | tf_op jit(solution)/shard_map/ppermute | solution.py:30
  60.2 4.7 %collective-permute-start.2 = (f32[16,512]{1,0:T(8,128)S(1)}, f32[16,512]{1,0:T(8,128)S(1)}, u32[]{:S(2)}, u32[]{:S(2)}) collective-permute-start(f32[16,512]{1,0:T(8,128)S(1)} %convert_reduce_fusion), channel_id=1, source_target_pairs={{0,64},{32,96},{64,0},{96,32},{128,192},{160,224},{192,128},{224,1... | collective-permute-start | bytes 98312 | tf_op jit(solution)/shard_map/ppermute | solution.py:30
  64.9 5.5 %collective-permute-start.3 = (f32[16,512]{1,0:T(8,128)S(1)}, f32[16,512]{1,0:T(8,128)S(1)}, u32[]{:S(2)}, u32[]{:S(2)}) collective-permute-start(f32[16,512]{1,0:T(8,128)S(1)} %add.18), channel_id=1, source_target_pairs={{0,192},{32,224},{64,128},{96,160},{128,64},{160,96},{192,0},{224,... | collective-permute-start | bytes 98312 | tf_op jit(solution)/shard_map/ppermute | solution.py:30
  70.4 5.2 %collective-permute-start.4 = (f32[16,512]{1,0:T(8,128)S(1)}, f32[16,512]{1,0:T(8,128)S(1)}, u32[]{:S(2)}, u32[]{:S(2)}) collective-permute-start(f32[16,512]{1,0:T(8,128)S(1)} %add_multiply_fusion), channel_id=1, source_target_pairs={{0,32},{32,0},{64,96},{96,64},{128,160},{160,128},{192,224},{224,1... | collective-permute-start | bytes 98312 | tf_op jit(solution)/shard_map/ppermute | solution.py:30
where the time goes:
time: 76.5 us; the launch traced here: 76.2 us
  blocking collectives  44.3 us (58%)
  starting transfers between devices  14.3 us (19%)
  Pallas kernels  11.4 us (15%)
  waiting for transfers between devices  3.9 us (5%)
  other arithmetic  0.89 us (1%)
    all_to_all x1, blocking collectives, shards(): received = lax.all_to_all(sent, 'col', 0, 0, tiled=True)  30.3 us
    ppermute x5, starting transfers between devices, exchange(): lax.ppermute(value, 'row', [(i, i ^ mask) for i in range(lax.axis_size('r...  14.3 us
    all_to_all x1, blocking collectives, shards(): lax.all_to_all(chip_sum.reshape(n_col, dim // n_col, dim), 'col', 0, 0, t...  14 us
    pallas_call x1, Pallas kernels, given_part(): pl.pallas_call(body, name='given_part', out_shape=(jax.ShapeDtypeStruct((...  3.94 us
    ppermute x5, waiting for transfers between devices, exchange(): lax.ppermute(value, 'row', [(i, i ^ mask) for i in range(lax.axis_size('r...  3.9 us
    pallas_call x1, Pallas kernels, load_columns(): pl.pallas_call(body, name='load_columns', out_shape=(jax.ShapeDtypeStruct...  2.3 us
    pallas_call x1, Pallas kernels, own_pairs(): pl.pallas_call(body, name='own_pairs', out_shape=(jax.ShapeDtypeStruct((c...  2.21 us
    pallas_call x1, Pallas kernels, kept_part(): pl.pallas_call(body, name='kept_part', out_shape=jax.ShapeDtypeStruct((di...  1.79 us
  transfers between devices with their start and end apart: 5, of which 4 were waited for; matrix products, arithmetic and copies ran while one was open for 0% of the time, Pallas kernels for 5%

commit v1 on v0

--- a/solution.py
+++ b/solution.py
@@ -10,7 +10,7 @@
 
 BF16, F32, I32 = jnp.bfloat16, jnp.float32, jnp.int32
 ROUND_ROWS = 32
-STEP_COLUMNS = 512
+STEP_COLUMNS = 256
 LOADS = 4
 
 in_vmem = functools.partial(pl.BlockSpec, memory_space=pltpu.VMEM)
@@ -49,14 +49,15 @@
     return jnp.sum(jnp.where(mine, panel_row + (1 - me * col_count), 0), axis=1, keepdims=True) - 1
 
 
-def load_columns(features, panel_row):
+def load_columns(features, panel_row, matrices):
     col_count, dim = features.shape
     count = panel_row.shape[1]
     bits = col_count.bit_length() - 1
     chunk = col_count // LOADS
     assert col_count == 1 << bits
 
-    def body(row_from, features_hbm, table, rounds, places, blank, row_ref, zeros, arrived):
+    def body(row_from, features_hbm, *refs):
+        matrix_rows, (table, rounds, places, tail, blank, row_ref, zeros, arrived) = refs[:2], refs[2:]
         row_load = pltpu.make_async_copy(row_from, row_ref, arrived.at[LOADS + 1])
         row_load.start()
         loads = []
@@ -64,6 +65,10 @@
             part = pl.ds(i * chunk, chunk)
             loads.append(pltpu.make_async_copy(features_hbm.at[part], table.at[part], arrived.at[i]))
             loads[i].start()
+        for core, source in enumerate(matrix_rows):
+            @pl.when(lax.axis_index("row") % 2 == core)
+            def _():
+                pltpu.make_async_copy(source, tail, arrived.at[LOADS + 2]).start()
         zeros[...] = jnp.zeros_like(zeros)
         loads.append(pltpu.make_async_copy(zeros, blank, arrived.at[LOADS]))
         loads[LOADS].start()
@@ -72,6 +77,7 @@
         owner_row, rank_row, _, _ = ranks(row, bits)
         rounds[0] = jnp.max(rank_row) // ROUND_ROWS + 1
         places[...] = jnp.broadcast_to(own_places(row, owner_row, rank_row, col_count, 0), (ROUND_ROWS, 128))
+        pltpu.make_async_copy(matrix_rows[0], tail, arrived.at[LOADS + 2]).wait()
         for load in loads:
             load.wait()
 
@@ -82,17 +88,18 @@
             jax.ShapeDtypeStruct(features.shape, BF16),
             jax.ShapeDtypeStruct((1,), I32),
             jax.ShapeDtypeStruct((ROUND_ROWS, 128), I32),
+            jax.ShapeDtypeStruct(matrices[0].shape, BF16),
             jax.ShapeDtypeStruct((count, dim), BF16),
         ),
-        in_specs=[in_place(), in_place()],
-        out_specs=(in_vmem(), in_smem(), in_vmem(), in_place()),
+        in_specs=[in_place()] * 4,
+        out_specs=(in_vmem(), in_smem(), in_vmem(), in_vmem(), in_place()),
         scratch_shapes=[
             pltpu.VMEM((1, count), I32),
             pltpu.VMEM((count, dim), BF16),
-            pltpu.SemaphoreType.DMA((LOADS + 2,)),
+            pltpu.SemaphoreType.DMA((LOADS + 3,)),
         ],
         compiler_params=params(),
-    )(panel_row, features)
+    )(panel_row, features, *matrices)
 
 
 def pack_rows(columns, panel_row, extra_rows, places, step):
@@ -104,11 +111,7 @@
     bits = col_count.bit_length() - 1
 
     def body(step_ref, row_ref, columns_ref, places_ref, *refs):
-        extra, (out, pick_out, tail, arrived) = refs[:-4], refs[-4:]
-        for core, source in enumerate(extra):
-            @pl.when(lax.axis_index("row") % 2 == core)
-            def _():
-                pltpu.make_async_copy(source, tail, arrived).start()
+        extra, (out, pick_out) = refs[:-2], refs[-2:]
         row, step = row_ref[...], step_ref[0]
         owner_row, rank_row, owner, rank = ranks(row, bits)
         wanted = places_ref[:, :1] if extra else own_places(row, owner_row, rank_row, col_count, step)
@@ -119,8 +122,7 @@
         pick = slot == lax.broadcasted_iota(I32, (count, n_slots), 1)
         pick_out[...] = pick.astype(F32).astype(BF16)
         if extra:
-            pltpu.make_async_copy(extra[0], tail, arrived).wait()
-            message = jnp.concatenate([message, tail[...]], axis=0)
+            message = jnp.concatenate([message, extra[0][...]], axis=0)
         for peer in range(n_col):
             out[peer] = message
 
@@ -131,9 +133,8 @@
             jax.ShapeDtypeStruct((n_col, ROUND_ROWS + n_extra, dim), BF16),
             jax.ShapeDtypeStruct((count, n_slots), BF16),
         ),
-        in_specs=[in_smem(), in_vmem(), in_vmem(), in_vmem()] + [in_place()] * len(extra_rows),
+        in_specs=[in_smem()] + [in_vmem()] * (3 + len(extra_rows)),
         out_specs=(in_vmem(), in_vmem()),
-        scratch_shapes=[pltpu.VMEM((max(n_extra, 16), dim), BF16), pltpu.SemaphoreType.DMA(())],
         compiler_params=params(),
     )(step, panel_row, columns, places, *extra_rows)
 
@@ -271,17 +272,22 @@
     )
     panel_row = panel_index.reshape(1, count)
     first = jnp.zeros((1,), I32)
-    columns, rounds, places, blank = load_columns(features, panel_row)
+    columns, rounds, places, matrix_rows, blank = load_columns(features, panel_row, (weight_raw, direction_raw))
 
     def another(state):
         step, rows = state
         message, pick = pack_rows(columns, panel_row, (), places, step)
         return step + 1, add_round(pick, lax.all_to_all(message, "col", 0, 0, tiled=True), rows)
 
-    _, later = lax.while_loop(lambda state: state[0][0] < rounds[0], another, (first + 1, blank))
+    later = lax.cond(
+        rounds[0] > 1,
+        lambda rows: lax.while_loop(lambda state: state[0][0] < rounds[0], another, (first + 1, rows))[1],
+        lambda rows: rows,
+        blank,
+    )
     panel_row, later = lax.optimization_barrier((panel_row, later))
     columns = pltpu.with_memory_space_constraint(columns, pltpu.VMEM)
-    sent, pick = pack_rows(columns, panel_row, (weight_raw, direction_raw), places, first)
+    sent, pick = pack_rows(columns, panel_row, (matrix_rows,), places, first)
     received = lax.all_to_all(sent, "col", 0, 0, tiled=True)
     kept_matrix = symmetric_matrix(received)
     other_matrix = exchange(kept_matrix, 1)

time: 76.5 us -> 76.1 us (level)
  no operation moved by 1% of the time
where the time goes in v1:
time: 76.1 us; the launch traced here: 75.8 us
  blocking collectives  44.2 us (58%)
  starting transfers between devices  14.3 us (19%)
  Pallas kernels  11.1 us (15%)
  waiting for transfers between devices  3.89 us (5%)
  between operations  1.37 us (2%)
  other arithmetic  0.89 us (1%)
    all_to_all x1, blocking collectives, shards(): received = lax.all_to_all(sent, 'col', 0, 0, tiled=True)  30.2 us
    ppermute x5, starting transfers between devices, exchange(): lax.ppermute(value, 'row', [(i, i ^ mask) for i in range(lax.axis_size('r...  14.3 us
    all_to_all x1, blocking collectives, shards(): lax.all_to_all(chip_sum.reshape(n_col, dim // n_col, dim), 'col', 0, 0, t...  14 us
    pallas_call x1, Pallas kernels, given_part(): pl.pallas_call(body, name='given_part', out_shape=(jax.ShapeDtypeStruct((...  3.92 us
    ppermute x5, waiting for transfers between devices, exchange(): lax.ppermute(value, 'row', [(i, i ^ mask) for i in range(lax.axis_size('r...  3.89 us
    pallas_call x1, Pallas kernels, own_pairs(): pl.pallas_call(body, name='own_pairs', out_shape=(jax.ShapeDtypeStruct((c...  2.21 us
    pallas_call x1, Pallas kernels, load_columns(): pl.pallas_call(body, name='load_columns', out_shape=(jax.ShapeDtypeStruct...  2.12 us
    pallas_call x1, Pallas kernels, kept_part(): pl.pallas_call(body, name='kept_part', out_shape=jax.ShapeDtypeStruct((di...  1.79 us
  transfers between devices with their start and end apart: 5, of which 4 were waited for; matrix products, arithmetic and copies ran while one was open for 0% of the time, Pallas kernels for 5%

profile of v1, /device:TPU:1, one launch (start us, length us, event | category | flops | bytes accessed | tf_op | source)
XLA Modules:
  0.0 75.8 jit_solution(11869713934044834275)
XLA Ops:
  0.6 0.0 copy-start.4
  0.6 2.1 %load_columns.1 = (bf16[2048,512]{1,0:T(8,128)(2,1)S(1)}, s32[1]{0:T(128)}, s32[32,128]{1,0:T(8,128)S(1)}, bf16[16,512]{1,0:T(8,128)(2,1)S(1)}, bf16[512,512]{1,0:T(8,128)(2,1)S(1)}) custom-call(s32[1,512]{1,0:T(1,128)} %bitcast.6, bf16[2048,512]{1,0:T(8,128)(2,1)} %features_hbm.1, bf16[16,512]{1,0:T(8,128)(2,1)} %refs_0_.1, bf16[16,512]{1,0:T(8,128)(2,1)} %refs_1_.1), custom_call_target="tpu_custom_call" | custom-call | tf_op jit(solution)/shard_map/load_columns/pallas_call | solution.py:84
  3.4 0.0 copy-done.4
  3.4 0.8 %pack_rows.2 = (bf16[32,48,512]{2,1,0:T(8,128)(2,1)S(1)}, bf16[512,1024]{1,0:T(8,128)(2,1)S(1)}) custom-call(s32[1]{0:T(128)} %constant.29.clone.1.step_ref, s32[1,512]{1,0:T(1,128)S(1)} %bitcast.8, bf16[2048,512]{1,0:T(8,128)(2,1)S(1)} %get-tuple-element.73.columns_ref, s32[32,128]{1,0:T(8,128)S(1)} %get-tuple-element.74.places_ref, ...), custom_call_target="tpu_custom_call" | custom-call | tf_op jit(solution)/shard_map/pack_rows/pallas_call | solution.py:129
  4.3 30.2 %all_to_all.15.received_ref = bf16[32,48,512]{2,1,0:T(8,128)(2,1)S(1)} all-to-all(bf16[32,48,512]{2,1,0:T(8,128)(2,1)S(1)} %get-tuple-element.78), channel_id=1, replica_groups=mesh['row'=8,'col'=32] {'col'}, dimensions={0} | all-to-all | bytes 3145728 | tf_op jit(solution)/shard_map/all_to_all | solution.py:291
  34.4 0.2 symmetric_matrix.1.matrix_ref
  34.7 2.7 %collective-permute-start = (bf16[512,512]{1,0:T(8,128)(2,1)S(1)}, bf16[512,512]{1,0:T(8,128)(2,1)S(1)}, u32[]{:S(2)}, u32[]{:S(2)}) collective-permute-start(bf16[512,512]{1,0:T(8,128)(2,1)S(1)} %symmetric_matrix.1.matrix_ref), channel_id=1, source_target_pairs={{0,32},{32,0},{64,96},{96,64},{128,160},{160,128},{192,224},{224,1... | collective-permute-start | bytes 1572872 | tf_op jit(solution)/shard_map/ppermute | solution.py:30
  37.4 2.2 %own_pairs.1 = (bf16[512,512]{1,0:T(8,128)(2,1)S(1)}, bf16[512,512]{1,0:T(8,128)(2,1)S(1)}, f32[512,2048]{1,0:T(8,128)S(1)}, s32[512,2048]{1,0:T(8,128)S(1)}) custom-call(bf16[512,1024]{1,0:T(8,128)(2,1)S(1)} %get-tuple-element.77.pick_ref, bf16[32,48,512]{2,1,0:T(8,128)(2,1)S(1)} %all_to_all.15.received_ref, ...), custom_call_target="tpu_custom_call" | custom-call | tf_op jit(solution)/shard_map/own_pairs/pallas_call | solution.py:201
  39.6 0.0 collective-permute-done.matrix_ref
  39.6 3.9 %given_part.1 = (bf16[512,512]{1,0:T(8,128)(2,1)S(1)}, bf16[512,2048]{1,0:T(8,128)(2,1)S(1)}) custom-call(bf16[512,512]{1,0:T(8,128)(2,1)S(1)} %get-tuple-element.81.panel_ref, bf16[512,512]{1,0:T(8,128)(2,1)S(1)} %get-tuple-element.80.turned_ref, bf16[512,512]{1,0:T(8,128)(2,1)S(1)} %collective-permute-done.matrix_ref, ...), custom_call_target="tpu_custom_call" | custom-call | tf_op jit(solution)/shard_map/given_part/pallas_call | solution.py:239
  43.5 0.1 collective-permute-start.1
  43.6 1.8 %kept_part.1 = f32[512,512]{1,0:T(8,128)S(1)} custom-call(bf16[512,512]{1,0:T(8,128)(2,1)S(1)} %get-tuple-element.80.turned_ref, bf16[512,2048]{1,0:T(8,128)(2,1)S(1)} %get-tuple-element.84.weights_ref, bf16[2048,512]{1,0:T(8,128)(2,1)S(1)} %get-tuple-element.73.columns_ref), custom_call_target="tpu_custom_call" | custom-call | tf_op jit(solution)/shard_map/kept_part/pallas_call | solution.py:256
  45.4 0.1 collective-permute-done.1
  45.5 0.2 add_convert_fusion
  45.7 14.0 %all_to_all.16 = bf16[32,16,512]{2,1,0:T(8,128)(2,1)S(1)} all-to-all(bf16[32,16,512]{2,1,0:T(8,128)(2,1)S(1)} %bitcast.5), channel_id=1, replica_groups=mesh['row'=8,'col'=32] {'col'}, dimensions={0} | all-to-all | bytes 1048576 | tf_op jit(solution)/shard_map/all_to_all | solution.py:299
  59.7 0.1 convert_reduce_fusion
  59.8 3.1 %collective-permute-start.2 = (f32[16,512]{1,0:T(8,128)S(1)}, f32[16,512]{1,0:T(8,128)S(1)}, u32[]{:S(2)}, u32[]{:S(2)}) collective-permute-start(f32[16,512]{1,0:T(8,128)S(1)} %convert_reduce_fusion), channel_id=1, source_target_pairs={{0,64},{32,96},{64,0},{96,32},{128,192},{160,224},{192,128},{224,1... | collective-permute-start | bytes 98312 | tf_op jit(solution)/shard_map/ppermute | solution.py:30
  62.9 1.6 %collective-permute-done.2 = f32[16,512]{1,0:T(8,128)S(1)} collective-permute-done((f32[16,512]{1,0:T(8,128)S(1)}, f32[16,512]{1,0:T(8,128)S(1)}, u32[]{:S(2)}, u32[]{:S(2)}) %collective-permute-start.2) | collective-permute-done | bytes 32800 | tf_op jit(solution)/shard_map/ppermute | solution.py:30
  64.5 4.2 %collective-permute-start.3 = (f32[16,512]{1,0:T(8,128)S(1)}, f32[16,512]{1,0:T(8,128)S(1)}, u32[]{:S(2)}, u32[]{:S(2)}) collective-permute-start(f32[16,512]{1,0:T(8,128)S(1)} %add.18), channel_id=1, source_target_pairs={{0,192},{32,224},{64,128},{96,160},{128,64},{160,96},{192,0},{224,... | collective-permute-start | bytes 98312 | tf_op jit(solution)/shard_map/ppermute | solution.py:30
  68.7 1.3 %collective-permute-done.3 = f32[16,512]{1,0:T(8,128)S(1)} collective-permute-done((f32[16,512]{1,0:T(8,128)S(1)}, f32[16,512]{1,0:T(8,128)S(1)}, u32[]{:S(2)}, u32[]{:S(2)}) %collective-permute-start.3) | collective-permute-done | bytes 32800 | tf_op jit(solution)/shard_map/ppermute | solution.py:30
  70.0 4.3 %collective-permute-start.4 = (f32[16,512]{1,0:T(8,128)S(1)}, f32[16,512]{1,0:T(8,128)S(1)}, u32[]{:S(2)}, u32[]{:S(2)}) collective-permute-start(f32[16,512]{1,0:T(8,128)S(1)} %add_multiply_fusion), channel_id=1, source_target_pairs={{0,32},{32,0},{64,96},{96,64},{128,160},{160,128},{192,224},{224,1... | collective-permute-start | bytes 98312 | tf_op jit(solution)/shard_map/ppermute | solution.py:30
  74.3 0.9 %collective-permute-done.4 = f32[16,512]{1,0:T(8,128)S(1)} collective-permute-done((f32[16,512]{1,0:T(8,128)S(1)}, f32[16,512]{1,0:T(8,128)S(1)}, u32[]{:S(2)}, u32[]{:S(2)}) %collective-permute-start.4) | collective-permute-done | bytes 32800 | tf_op jit(solution)/shard_map/ppermute | solution.py:30
  75.2 0.6 broadcast_select_fusion
  (3 shorter events, 0.0 us)
Async XLA Ops:
  0.6 2.8 %copy-start.4 = (s32[512]{0:T(512)S(1)}, s32[512]{0:T(512)}, u32[]{:S(2)}) copy-start(s32[512]{0:T(512)} %param.12) | copy-start | bytes 6148
  34.7 4.9 %collective-permute-start = (bf16[512,512]{1,0:T(8,128)(2,1)S(1)}, bf16[512,512]{1,0:T(8,128)(2,1)S(1)}, u32[]{:S(2)}, u32[]{:S(2)}) collective-permute-start(bf16[512,512]{1,0:T(8,128)(2,1)S(1)} %symmetric_matrix.1.matrix_ref), channel_id=1, source_target_pairs={{0,32},{32,0},{64,96},{96,64},{128,160},{160,128},{192,224},{224,1... | collective-permute-start | bytes 1572872 | tf_op jit(solution)/shard_map/ppermute | solution.py:30
  43.5 2.0 %collective-permute-start.1 = (bf16[512,512]{1,0:T(8,128)(2,1)S(1)}, bf16[512,512]{1,0:T(8,128)(2,1)S(1)}, u32[]{:S(2)}, u32[]{:S(2)}) collective-permute-start(bf16[512,512]{1,0:T(8,128)(2,1)S(1)} %get-tuple-element.85), channel_id=1, source_target_pairs={{0,32},{32,0},{64,96},{96,64},{128,160},{160,128},{192,224},{224,1... | collective-permute-start | bytes 1572872 | tf_op jit(solution)/shard_map/ppermute | solution.py:30
  59.8 4.7 %collective-permute-start.2 = (f32[16,512]{1,0:T(8,128)S(1)}, f32[16,512]{1,0:T(8,128)S(1)}, u32[]{:S(2)}, u32[]{:S(2)}) collective-permute-start(f32[16,512]{1,0:T(8,128)S(1)} %convert_reduce_fusion), channel_id=1, source_target_pairs={{0,64},{32,96},{64,0},{96,32},{128,192},{160,224},{192,128},{224,1... | collective-permute-start | bytes 98312 | tf_op jit(solution)/shard_map/ppermute | solution.py:30
  64.5 5.5 %collective-permute-start.3 = (f32[16,512]{1,0:T(8,128)S(1)}, f32[16,512]{1,0:T(8,128)S(1)}, u32[]{:S(2)}, u32[]{:S(2)}) collective-permute-start(f32[16,512]{1,0:T(8,128)S(1)} %add.18), channel_id=1, source_target_pairs={{0,192},{32,224},{64,128},{96,160},{128,64},{160,96},{192,0},{224,... | collective-permute-start | bytes 98312 | tf_op jit(solution)/shard_map/ppermute | solution.py:30
  70.0 5.2 %collective-permute-start.4 = (f32[16,512]{1,0:T(8,128)S(1)}, f32[16,512]{1,0:T(8,128)S(1)}, u32[]{:S(2)}, u32[]{:S(2)}) collective-permute-start(f32[16,512]{1,0:T(8,128)S(1)} %add_multiply_fusion), channel_id=1, source_target_pairs={{0,32},{32,0},{64,96},{96,64},{128,160},{160,128},{192,224},{224,1... | collective-permute-start | bytes 98312 | tf_op jit(solution)/shard_map/ppermute | solution.py:30

commit v2 on v1

--- a/solution.py
+++ b/solution.py
@@ -57,7 +57,7 @@
     assert col_count == 1 << bits
 
     def body(row_from, features_hbm, *refs):
-        matrix_rows, (table, rounds, places, tail, blank, row_ref, zeros, arrived) = refs[:2], refs[2:]
+        matrix_rows, (table, rounds, places, where, tail, blank, row_ref, zeros, arrived) = refs[:2], refs[2:]
         row_load = pltpu.make_async_copy(row_from, row_ref, arrived.at[LOADS + 1])
         row_load.start()
         loads = []
@@ -74,7 +74,8 @@
         loads[LOADS].start()
         row_load.wait()
         row = row_ref[...]
-        owner_row, rank_row, _, _ = ranks(row, bits)
+        owner_row, rank_row, owner, rank = ranks(row, bits)
+        where[...] = jnp.where(lax.broadcasted_iota(I32, (count, 128), 1) == 0, owner, rank)
         rounds[0] = jnp.max(rank_row) // ROUND_ROWS + 1
         places[...] = jnp.broadcast_to(own_places(row, owner_row, rank_row, col_count, 0), (ROUND_ROWS, 128))
         pltpu.make_async_copy(matrix_rows[0], tail, arrived.at[LOADS + 2]).wait()
@@ -88,11 +89,12 @@
             jax.ShapeDtypeStruct(features.shape, BF16),
             jax.ShapeDtypeStruct((1,), I32),
             jax.ShapeDtypeStruct((ROUND_ROWS, 128), I32),
+            jax.ShapeDtypeStruct((count, 128), I32),
             jax.ShapeDtypeStruct(matrices[0].shape, BF16),
             jax.ShapeDtypeStruct((count, dim), BF16),
         ),
         in_specs=[in_place()] * 4,
-        out_specs=(in_vmem(), in_smem(), in_vmem(), in_vmem(), in_place()),
+        out_specs=(in_vmem(), in_smem(), in_vmem(), in_vmem(), in_vmem(), in_place()),
         scratch_shapes=[
             pltpu.VMEM((1, count), I32),
             pltpu.VMEM((count, dim), BF16),
@@ -102,7 +104,7 @@
     )(panel_row, features, *matrices)
 
 
-def pack_rows(columns, panel_row, extra_rows, places, step):
+def pack_rows(columns, panel_row, extra_rows, places, where, step):
     n_col = lax.axis_size("col")
     n_slots = n_col * ROUND_ROWS
     col_count, dim = columns.shape
@@ -110,14 +112,17 @@
     n_extra = extra_rows[0].shape[0] if extra_rows else 0
     bits = col_count.bit_length() - 1
 
-    def body(step_ref, row_ref, columns_ref, places_ref, *refs):
+    def body(step_ref, row_ref, columns_ref, places_ref, where_ref, *refs):
         extra, (out, pick_out) = refs[:-2], refs[-2:]
-        row, step = row_ref[...], step_ref[0]
-        owner_row, rank_row, owner, rank = ranks(row, bits)
-        wanted = places_ref[:, :1] if extra else own_places(row, owner_row, rank_row, col_count, step)
+        step = step_ref[0]
+        if extra:
+            wanted = places_ref[:, :1]
+        else:
+            owner_row, rank_row, _, _ = ranks(row_ref[...], bits)
+            wanted = own_places(row_ref[...], owner_row, rank_row, col_count, step)
         chosen = (wanted == lax.broadcasted_iota(I32, (ROUND_ROWS, col_count), 1)).astype(F32).astype(BF16)
         message = rows_of(chosen, columns_ref[...]).astype(BF16)
-        rank = rank - step * ROUND_ROWS
+        owner, rank = where_ref[:, :1], where_ref[:, 1:2] - step * ROUND_ROWS
         slot = jnp.where((rank >= 0) & (rank < ROUND_ROWS), owner * ROUND_ROWS + rank, -1)
         pick = slot == lax.broadcasted_iota(I32, (count, n_slots), 1)
         pick_out[...] = pick.astype(F32).astype(BF16)
@@ -133,10 +138,10 @@
             jax.ShapeDtypeStruct((n_col, ROUND_ROWS + n_extra, dim), BF16),
             jax.ShapeDtypeStruct((count, n_slots), BF16),
         ),
-        in_specs=[in_smem()] + [in_vmem()] * (3 + len(extra_rows)),
+        in_specs=[in_smem()] + [in_vmem()] * (4 + len(extra_rows)),
         out_specs=(in_vmem(), in_vmem()),
         compiler_params=params(),
-    )(step, panel_row, columns, places, *extra_rows)
+    )(step, panel_row, columns, places, where, *extra_rows)
 
 
 def panel_part(received):
@@ -272,11 +277,11 @@
     )
     panel_row = panel_index.reshape(1, count)
     first = jnp.zeros((1,), I32)
-    columns, rounds, places, matrix_rows, blank = load_columns(features, panel_row, (weight_raw, direction_raw))
+    columns, rounds, places, where, matrix_rows, blank = load_columns(features, panel_row, (weight_raw, direction_raw))
 
     def another(state):
         step, rows = state
-        message, pick = pack_rows(columns, panel_row, (), places, step)
+        message, pick = pack_rows(columns, panel_row, (), places, where, step)
         return step + 1, add_round(pick, lax.all_to_all(message, "col", 0, 0, tiled=True), rows)
 
     later = lax.cond(
@@ -287,7 +292,7 @@
     )
     panel_row, later = lax.optimization_barrier((panel_row, later))
     columns = pltpu.with_memory_space_constraint(columns, pltpu.VMEM)
-    sent, pick = pack_rows(columns, panel_row, (matrix_rows,), places, first)
+    sent, pick = pack_rows(columns, panel_row, (matrix_rows,), places, where, first)
     received = lax.all_to_all(sent, "col", 0, 0, tiled=True)
     kept_matrix = symmetric_matrix(received)
     other_matrix = exchange(kept_matrix, 1)

time: 76.1 us -> 75.9 us (level)
  no operation moved by 1% of the time
where the time goes in v2:
time: 75.9 us; the launch traced here: 75.6 us
  blocking collectives  44.2 us (58%)
  starting transfers between devices  14.3 us (19%)
  Pallas kernels  11 us (14%)
  waiting for transfers between devices  3.89 us (5%)
  between operations  1.37 us (2%)
  other arithmetic  0.89 us (1%)
    all_to_all x1, blocking collectives, shards(): received = lax.all_to_all(sent, 'col', 0, 0, tiled=True)  30.2 us
    ppermute x5, starting transfers between devices, exchange(): lax.ppermute(value, 'row', [(i, i ^ mask) for i in range(lax.axis_size('r...  14.3 us
    all_to_all x1, blocking collectives, shards(): lax.all_to_all(chip_sum.reshape(n_col, dim // n_col, dim), 'col', 0, 0, t...  14 us
    pallas_call x1, Pallas kernels, given_part(): pl.pallas_call(body, name='given_part', out_shape=(jax.ShapeDtypeStruct((...  3.93 us
    ppermute x5, waiting for transfers between devices, exchange(): lax.ppermute(value, 'row', [(i, i ^ mask) for i in range(lax.axis_size('r...  3.89 us
    pallas_call x1, Pallas kernels, own_pairs(): pl.pallas_call(body, name='own_pairs', out_shape=(jax.ShapeDtypeStruct((c...  2.21 us
    pallas_call x1, Pallas kernels, load_columns(): pl.pallas_call(body, name='load_columns', out_shape=(jax.ShapeDtypeStruct...  2.12 us
    pallas_call x1, Pallas kernels, kept_part(): pl.pallas_call(body, name='kept_part', out_shape=jax.ShapeDtypeStruct((di...  1.79 us
  transfers between devices with their start and end apart: 5, of which 4 were waited for; matrix products, arithmetic and copies ran while one was open for 0% of the time, Pallas kernels for 5%

profile of v2, /device:TPU:1, one launch (start us, length us, event | category | flops | bytes accessed | tf_op | source)
XLA Modules:
  0.0 75.6 jit_solution(16110912248051557190)
XLA Ops:
  0.6 0.0 copy-start.4
  0.6 2.1 %load_columns.1 = (bf16[2048,512]{1,0:T(8,128)(2,1)S(1)}, s32[1]{0:T(128)}, s32[32,128]{1,0:T(8,128)S(1)}, s32[512,128]{1,0:T(8,128)S(1)}, bf16[16,512]{1,0:T(8,128)(2,1)S(1)}, /*index=5*/bf16[512,512]{1,0:T(8,128)(2,1)S(1)}) custom-call(s32[1,512]{1,0:T(1,128)} %bitcast.6, bf16[2048,512]{1,0:T(8,128)(2,1)} %features_hbm.1, bf16[16,512]{1,0:T(8,128)(2,1)} %refs_0_.1, ...), custom_call_target="tpu_custom_call" | custom-call | tf_op jit(solution)/shard_map/load_columns/pallas_call | solution.py:85
  3.4 0.0 copy-done.4
  3.4 0.7 pack_rows.2
  4.1 30.2 %all_to_all.15.received_ref = bf16[32,48,512]{2,1,0:T(8,128)(2,1)S(1)} all-to-all(bf16[32,48,512]{2,1,0:T(8,128)(2,1)S(1)} %get-tuple-element.88), channel_id=1, replica_groups=mesh['row'=8,'col'=32] {'col'}, dimensions={0} | all-to-all | bytes 3145728 | tf_op jit(solution)/shard_map/all_to_all | solution.py:296
  34.3 0.2 symmetric_matrix.1.matrix_ref
  34.5 2.7 %collective-permute-start = (bf16[512,512]{1,0:T(8,128)(2,1)S(1)}, bf16[512,512]{1,0:T(8,128)(2,1)S(1)}, u32[]{:S(2)}, u32[]{:S(2)}) collective-permute-start(bf16[512,512]{1,0:T(8,128)(2,1)S(1)} %symmetric_matrix.1.matrix_ref), channel_id=1, source_target_pairs={{0,32},{32,0},{64,96},{96,64},{128,160},{160,128},{192,224},{224,1... | collective-permute-start | bytes 1572872 | tf_op jit(solution)/shard_map/ppermute | solution.py:30
  37.2 2.2 %own_pairs.1 = (bf16[512,512]{1,0:T(8,128)(2,1)S(1)}, bf16[512,512]{1,0:T(8,128)(2,1)S(1)}, f32[512,2048]{1,0:T(8,128)S(1)}, s32[512,2048]{1,0:T(8,128)S(1)}) custom-call(bf16[512,1024]{1,0:T(8,128)(2,1)S(1)} %get-tuple-element.87.pick_ref, bf16[32,48,512]{2,1,0:T(8,128)(2,1)S(1)} %all_to_all.15.received_ref, ...), custom_call_target="tpu_custom_call" | custom-call | tf_op jit(solution)/shard_map/own_pairs/pallas_call | solution.py:206
  39.4 0.0 collective-permute-done.matrix_ref
  39.4 3.9 %given_part.1 = (bf16[512,512]{1,0:T(8,128)(2,1)S(1)}, bf16[512,2048]{1,0:T(8,128)(2,1)S(1)}) custom-call(bf16[512,512]{1,0:T(8,128)(2,1)S(1)} %get-tuple-element.91.panel_ref, bf16[512,512]{1,0:T(8,128)(2,1)S(1)} %get-tuple-element.90.turned_ref, bf16[512,512]{1,0:T(8,128)(2,1)S(1)} %collective-permute-done.matrix_ref, ...), custom_call_target="tpu_custom_call" | custom-call | tf_op jit(solution)/shard_map/given_part/pallas_call | solution.py:244
  43.4 0.1 collective-permute-start.1
  43.5 1.8 %kept_part.1 = f32[512,512]{1,0:T(8,128)S(1)} custom-call(bf16[512,512]{1,0:T(8,128)(2,1)S(1)} %get-tuple-element.90.turned_ref, bf16[512,2048]{1,0:T(8,128)(2,1)S(1)} %get-tuple-element.94.weights_ref, bf16[2048,512]{1,0:T(8,128)(2,1)S(1)} %get-tuple-element.82.columns_ref), custom_call_target="tpu_custom_call" | custom-call | tf_op jit(solution)/shard_map/kept_part/pallas_call | solution.py:261
  45.3 0.1 collective-permute-done.1
  45.4 0.2 add_convert_fusion
  45.5 14.0 %all_to_all.16 = bf16[32,16,512]{2,1,0:T(8,128)(2,1)S(1)} all-to-all(bf16[32,16,512]{2,1,0:T(8,128)(2,1)S(1)} %bitcast.5), channel_id=1, replica_groups=mesh['row'=8,'col'=32] {'col'}, dimensions={0} | all-to-all | bytes 1048576 | tf_op jit(solution)/shard_map/all_to_all | solution.py:304
  59.6 0.1 convert_reduce_fusion
  59.6 3.1 %collective-permute-start.2 = (f32[16,512]{1,0:T(8,128)S(1)}, f32[16,512]{1,0:T(8,128)S(1)}, u32[]{:S(2)}, u32[]{:S(2)}) collective-permute-start(f32[16,512]{1,0:T(8,128)S(1)} %convert_reduce_fusion), channel_id=1, source_target_pairs={{0,64},{32,96},{64,0},{96,32},{128,192},{160,224},{192,128},{224,1... | collective-permute-start | bytes 98312 | tf_op jit(solution)/shard_map/ppermute | solution.py:30
  62.7 1.6 %collective-permute-done.2 = f32[16,512]{1,0:T(8,128)S(1)} collective-permute-done((f32[16,512]{1,0:T(8,128)S(1)}, f32[16,512]{1,0:T(8,128)S(1)}, u32[]{:S(2)}, u32[]{:S(2)}) %collective-permute-start.2) | collective-permute-done | bytes 32800 | tf_op jit(solution)/shard_map/ppermute | solution.py:30
  64.4 4.1 %collective-permute-start.3 = (f32[16,512]{1,0:T(8,128)S(1)}, f32[16,512]{1,0:T(8,128)S(1)}, u32[]{:S(2)}, u32[]{:S(2)}) collective-permute-start(f32[16,512]{1,0:T(8,128)S(1)} %add.18), channel_id=1, source_target_pairs={{0,192},{32,224},{64,128},{96,160},{128,64},{160,96},{192,0},{224,... | collective-permute-start | bytes 98312 | tf_op jit(solution)/shard_map/ppermute | solution.py:30
  68.5 1.3 %collective-permute-done.3 = f32[16,512]{1,0:T(8,128)S(1)} collective-permute-done((f32[16,512]{1,0:T(8,128)S(1)}, f32[16,512]{1,0:T(8,128)S(1)}, u32[]{:S(2)}, u32[]{:S(2)}) %collective-permute-start.3) | collective-permute-done | bytes 32800 | tf_op jit(solution)/shard_map/ppermute | solution.py:30
  69.8 4.3 %collective-permute-start.4 = (f32[16,512]{1,0:T(8,128)S(1)}, f32[16,512]{1,0:T(8,128)S(1)}, u32[]{:S(2)}, u32[]{:S(2)}) collective-permute-start(f32[16,512]{1,0:T(8,128)S(1)} %add_multiply_fusion), channel_id=1, source_target_pairs={{0,32},{32,0},{64,96},{96,64},{128,160},{160,128},{192,224},{224,1... | collective-permute-start | bytes 98312 | tf_op jit(solution)/shard_map/ppermute | solution.py:30
  74.1 0.9 %collective-permute-done.4 = f32[16,512]{1,0:T(8,128)S(1)} collective-permute-done((f32[16,512]{1,0:T(8,128)S(1)}, f32[16,512]{1,0:T(8,128)S(1)}, u32[]{:S(2)}, u32[]{:S(2)}) %collective-permute-start.4) | collective-permute-done | bytes 32800 | tf_op jit(solution)/shard_map/ppermute | solution.py:30
  75.0 0.6 broadcast_select_fusion
  (3 shorter events, 0.0 us)
Async XLA Ops:
  0.6 2.8 %copy-start.4 = (s32[512]{0:T(512)S(1)}, s32[512]{0:T(512)}, u32[]{:S(2)}) copy-start(s32[512]{0:T(512)} %param.12) | copy-start | bytes 6148
  34.5 4.9 %collective-permute-start = (bf16[512,512]{1,0:T(8,128)(2,1)S(1)}, bf16[512,512]{1,0:T(8,128)(2,1)S(1)}, u32[]{:S(2)}, u32[]{:S(2)}) collective-permute-start(bf16[512,512]{1,0:T(8,128)(2,1)S(1)} %symmetric_matrix.1.matrix_ref), channel_id=1, source_target_pairs={{0,32},{32,0},{64,96},{96,64},{128,160},{160,128},{192,224},{224,1... | collective-permute-start | bytes 1572872 | tf_op jit(solution)/shard_map/ppermute | solution.py:30
  43.4 2.0 %collective-permute-start.1 = (bf16[512,512]{1,0:T(8,128)(2,1)S(1)}, bf16[512,512]{1,0:T(8,128)(2,1)S(1)}, u32[]{:S(2)}, u32[]{:S(2)}) collective-permute-start(bf16[512,512]{1,0:T(8,128)(2,1)S(1)} %get-tuple-element.95), channel_id=1, source_target_pairs={{0,32},{32,0},{64,96},{96,64},{128,160},{160,128},{192,224},{224,1... | collective-permute-start | bytes 1572872 | tf_op jit(solution)/shard_map/ppermute | solution.py:30
  59.6 4.7 %collective-permute-start.2 = (f32[16,512]{1,0:T(8,128)S(1)}, f32[16,512]{1,0:T(8,128)S(1)}, u32[]{:S(2)}, u32[]{:S(2)}) collective-permute-start(f32[16,512]{1,0:T(8,128)S(1)} %convert_reduce_fusion), channel_id=1, source_target_pairs={{0,64},{32,96},{64,0},{96,32},{128,192},{160,224},{192,128},{224,1... | collective-permute-start | bytes 98312 | tf_op jit(solution)/shard_map/ppermute | solution.py:30
  64.4 5.5 %collective-permute-start.3 = (f32[16,512]{1,0:T(8,128)S(1)}, f32[16,512]{1,0:T(8,128)S(1)}, u32[]{:S(2)}, u32[]{:S(2)}) collective-permute-start(f32[16,512]{1,0:T(8,128)S(1)} %add.18), channel_id=1, source_target_pairs={{0,192},{32,224},{64,128},{96,160},{128,64},{160,96},{192,0},{224,... | collective-permute-start | bytes 98312 | tf_op jit(solution)/shard_map/ppermute | solution.py:30
  69.8 5.2 %collective-permute-start.4 = (f32[16,512]{1,0:T(8,128)S(1)}, f32[16,512]{1,0:T(8,128)S(1)}, u32[]{:S(2)}, u32[]{:S(2)}) collective-permute-start(f32[16,512]{1,0:T(8,128)S(1)} %add_multiply_fusion), channel_id=1, source_target_pairs={{0,32},{32,0},{64,96},{96,64},{128,160},{160,128},{192,224},{224,1... | collective-permute-start | bytes 98312 | tf_op jit(solution)/shard_map/ppermute | solution.py:30

commit v3 on v2

--- a/solution.py
+++ b/solution.py
@@ -10,7 +10,7 @@
 
 BF16, F32, I32 = jnp.bfloat16, jnp.float32, jnp.int32
 ROUND_ROWS = 32
-STEP_COLUMNS = 256
+STEP_ROWS = 256
 LOADS = 4
 
 in_vmem = functools.partial(pl.BlockSpec, memory_space=pltpu.VMEM)
@@ -223,23 +223,25 @@
     count, dim = panel.shape
     col_count = columns.shape[0]
 
-    def body(panel_ref, turned_ref, matrix_ref, own_ref, columns_ref, labels_ref, given, kept_weights, weights):
+    def body(panel_ref, turned_ref, matrix_ref, own_ref, columns_ref, labels_ref, given, kept_weights, sums):
         first = lax.axis_index("row") % 2 == 0
         projected = rows_of(panel_ref[...], matrix_ref[...]).astype(BF16)
-        for start in range(0, col_count, STEP_COLUMNS):
-            part = pl.ds(start, STEP_COLUMNS)
+        columns = columns_ref[...]
+        for start in range(0, count, STEP_ROWS):
+            part = pl.ds(start, STEP_ROWS)
             other = lax.dot_general(
-                projected, columns_ref[part], (((1,), (1,)), ((), ())), preferred_element_type=F32
+                projected[start : start + STEP_ROWS], columns, (((1,), (1,)), ((), ())), preferred_element_type=F32
             )
-            mine = own_ref[:, part]
+            mine = own_ref[part]
             margin = jnp.where(first, mine, other)
             change = jnp.where(first, other, mine)
             probability = 1.0 / (1.0 + jnp.exp(-margin))
-            residual = probability - labels_ref[:, part].astype(F32)
+            residual = probability - labels_ref[part].astype(F32)
             curvature = probability * (1.0 - probability) * change
-            kept_weights[:, part] = jnp.where(first, residual, curvature).astype(BF16)
-            weights[:, part] = jnp.where(first, curvature, residual).astype(BF16)
-        given[...] = panel_product(turned_ref[...], weights[...], columns_ref[...]).astype(BF16)
+            kept_weights[part] = jnp.where(first, residual, curvature).astype(BF16)
+            sums[part] = rows_of(jnp.where(first, curvature, residual).astype(BF16), columns).astype(BF16)
+        half = rows_of(turned_ref[...], sums[...])
+        given[...] = (half + half.T).astype(BF16)
 
     return pl.pallas_call(
         body,
@@ -247,7 +249,7 @@
         out_shape=(jax.ShapeDtypeStruct((dim, dim), BF16), jax.ShapeDtypeStruct((count, col_count), BF16)),
         in_specs=[in_vmem()] * 6,
         out_specs=(in_vmem(), in_vmem()),
-        scratch_shapes=[pltpu.VMEM((count, col_count), BF16)],
+        scratch_shapes=[pltpu.VMEM((count, dim), BF16)],
         compiler_params=params(16),
     )(panel, turned, other_matrix, own, columns, labels)
 

time: 75.9 us -> 76.2 us (level)
  no operation moved by 1% of the time
where the time goes in v3:
time: 76.2 us; the launch traced here: 75.9 us
  blocking collectives  44.2 us (58%)
  starting transfers between devices  14.3 us (19%)
  Pallas kernels  11.2 us (15%)
  waiting for transfers between devices  3.89 us (5%)
  between operations  1.37 us (2%)
  other arithmetic  0.89 us (1%)
    all_to_all x1, blocking collectives, shards(): received = lax.all_to_all(sent, 'col', 0, 0, tiled=True)  30.2 us
    ppermute x5, starting transfers between devices, exchange(): lax.ppermute(value, 'row', [(i, i ^ mask) for i in range(lax.axis_size('r...  14.3 us
    all_to_all x1, blocking collectives, shards(): lax.all_to_all(chip_sum.reshape(n_col, dim // n_col, dim), 'col', 0, 0, t...  14 us
    pallas_call x1, Pallas kernels, given_part(): pl.pallas_call(body, name='given_part', out_shape=(jax.ShapeDtypeStruct((...  4.2 us
    ppermute x5, waiting for transfers between devices, exchange(): lax.ppermute(value, 'row', [(i, i ^ mask) for i in range(lax.axis_size('r...  3.89 us
    pallas_call x1, Pallas kernels, own_pairs(): pl.pallas_call(body, name='own_pairs', out_shape=(jax.ShapeDtypeStruct((c...  2.21 us
    pallas_call x1, Pallas kernels, load_columns(): pl.pallas_call(body, name='load_columns', out_shape=(jax.ShapeDtypeStruct...  2.12 us
    pallas_call x1, Pallas kernels, kept_part(): pl.pallas_call(body, name='kept_part', out_shape=jax.ShapeDtypeStruct((di...  1.79 us
  transfers between devices with their start and end apart: 5, of which 4 were waited for; matrix products, arithmetic and copies ran while one was open for 0% of the time, Pallas kernels for 5%

profile of v3, /device:TPU:1, one launch (start us, length us, event | category | flops | bytes accessed | tf_op | source)
XLA Modules:
  0.0 75.9 jit_solution(8787116173039135395)
XLA Ops:
  0.6 0.0 copy-start.4
  0.6 2.1 %load_columns.1 = (bf16[2048,512]{1,0:T(8,128)(2,1)S(1)}, s32[1]{0:T(128)}, s32[32,128]{1,0:T(8,128)S(1)}, s32[512,128]{1,0:T(8,128)S(1)}, bf16[16,512]{1,0:T(8,128)(2,1)S(1)}, /*index=5*/bf16[512,512]{1,0:T(8,128)(2,1)S(1)}) custom-call(s32[1,512]{1,0:T(1,128)} %bitcast.6, bf16[2048,512]{1,0:T(8,128)(2,1)} %features_hbm.1, bf16[16,512]{1,0:T(8,128)(2,1)} %refs_0_.1, ...), custom_call_target="tpu_custom_call" | custom-call | tf_op jit(solution)/shard_map/load_columns/pallas_call | solution.py:85
  3.4 0.0 copy-done.4
  3.4 0.7 pack_rows.2
  4.1 30.2 %all_to_all.15.received_ref = bf16[32,48,512]{2,1,0:T(8,128)(2,1)S(1)} all-to-all(bf16[32,48,512]{2,1,0:T(8,128)(2,1)S(1)} %get-tuple-element.88), channel_id=1, replica_groups=mesh['row'=8,'col'=32] {'col'}, dimensions={0} | all-to-all | bytes 3145728 | tf_op jit(solution)/shard_map/all_to_all | solution.py:298
  34.3 0.2 symmetric_matrix.1.matrix_ref
  34.5 2.7 %collective-permute-start = (bf16[512,512]{1,0:T(8,128)(2,1)S(1)}, bf16[512,512]{1,0:T(8,128)(2,1)S(1)}, u32[]{:S(2)}, u32[]{:S(2)}) collective-permute-start(bf16[512,512]{1,0:T(8,128)(2,1)S(1)} %symmetric_matrix.1.matrix_ref), channel_id=1, source_target_pairs={{0,32},{32,0},{64,96},{96,64},{128,160},{160,128},{192,224},{224,1... | collective-permute-start | bytes 1572872 | tf_op jit(solution)/shard_map/ppermute | solution.py:30
  37.2 2.2 %own_pairs.1 = (bf16[512,512]{1,0:T(8,128)(2,1)S(1)}, bf16[512,512]{1,0:T(8,128)(2,1)S(1)}, f32[512,2048]{1,0:T(8,128)S(1)}, s32[512,2048]{1,0:T(8,128)S(1)}) custom-call(bf16[512,1024]{1,0:T(8,128)(2,1)S(1)} %get-tuple-element.87.pick_ref, bf16[32,48,512]{2,1,0:T(8,128)(2,1)S(1)} %all_to_all.15.received_ref, ...), custom_call_target="tpu_custom_call" | custom-call | tf_op jit(solution)/shard_map/own_pairs/pallas_call | solution.py:206
  39.4 0.0 collective-permute-done.matrix_ref
  39.4 4.2 %given_part.1 = (bf16[512,512]{1,0:T(8,128)(2,1)S(1)}, bf16[512,2048]{1,0:T(8,128)(2,1)S(1)}) custom-call(bf16[512,512]{1,0:T(8,128)(2,1)S(1)} %get-tuple-element.91.panel_ref, bf16[512,512]{1,0:T(8,128)(2,1)S(1)} %get-tuple-element.90.turned_ref, bf16[512,512]{1,0:T(8,128)(2,1)S(1)} %collective-permute-done.matrix_ref, ...), custom_call_target="tpu_custom_call" | custom-call | tf_op jit(solution)/shard_map/given_part/pallas_call | solution.py:246
  43.6 0.1 collective-permute-start.1
  43.7 1.8 %kept_part.1 = f32[512,512]{1,0:T(8,128)S(1)} custom-call(bf16[512,512]{1,0:T(8,128)(2,1)S(1)} %get-tuple-element.90.turned_ref, bf16[512,2048]{1,0:T(8,128)(2,1)S(1)} %get-tuple-element.94.weights_ref, bf16[2048,512]{1,0:T(8,128)(2,1)S(1)} %get-tuple-element.82.columns_ref), custom_call_target="tpu_custom_call" | custom-call | tf_op jit(solution)/shard_map/kept_part/pallas_call | solution.py:263
  45.5 0.1 collective-permute-done.1
  45.6 0.2 add_convert_fusion
  45.8 14.0 %all_to_all.16 = bf16[32,16,512]{2,1,0:T(8,128)(2,1)S(1)} all-to-all(bf16[32,16,512]{2,1,0:T(8,128)(2,1)S(1)} %bitcast.5), channel_id=1, replica_groups=mesh['row'=8,'col'=32] {'col'}, dimensions={0} | all-to-all | bytes 1048576 | tf_op jit(solution)/shard_map/all_to_all | solution.py:306
  59.8 0.1 convert_reduce_fusion
  59.9 3.1 %collective-permute-start.2 = (f32[16,512]{1,0:T(8,128)S(1)}, f32[16,512]{1,0:T(8,128)S(1)}, u32[]{:S(2)}, u32[]{:S(2)}) collective-permute-start(f32[16,512]{1,0:T(8,128)S(1)} %convert_reduce_fusion), channel_id=1, source_target_pairs={{0,64},{32,96},{64,0},{96,32},{128,192},{160,224},{192,128},{224,1... | collective-permute-start | bytes 98312 | tf_op jit(solution)/shard_map/ppermute | solution.py:30
  63.0 1.6 %collective-permute-done.2 = f32[16,512]{1,0:T(8,128)S(1)} collective-permute-done((f32[16,512]{1,0:T(8,128)S(1)}, f32[16,512]{1,0:T(8,128)S(1)}, u32[]{:S(2)}, u32[]{:S(2)}) %collective-permute-start.2) | collective-permute-done | bytes 32800 | tf_op jit(solution)/shard_map/ppermute | solution.py:30
  64.6 4.2 %collective-permute-start.3 = (f32[16,512]{1,0:T(8,128)S(1)}, f32[16,512]{1,0:T(8,128)S(1)}, u32[]{:S(2)}, u32[]{:S(2)}) collective-permute-start(f32[16,512]{1,0:T(8,128)S(1)} %add.18), channel_id=1, source_target_pairs={{0,192},{32,224},{64,128},{96,160},{128,64},{160,96},{192,0},{224,... | collective-permute-start | bytes 98312 | tf_op jit(solution)/shard_map/ppermute | solution.py:30
  68.8 1.3 %collective-permute-done.3 = f32[16,512]{1,0:T(8,128)S(1)} collective-permute-done((f32[16,512]{1,0:T(8,128)S(1)}, f32[16,512]{1,0:T(8,128)S(1)}, u32[]{:S(2)}, u32[]{:S(2)}) %collective-permute-start.3) | collective-permute-done | bytes 32800 | tf_op jit(solution)/shard_map/ppermute | solution.py:30
  70.1 4.3 %collective-permute-start.4 = (f32[16,512]{1,0:T(8,128)S(1)}, f32[16,512]{1,0:T(8,128)S(1)}, u32[]{:S(2)}, u32[]{:S(2)}) collective-permute-start(f32[16,512]{1,0:T(8,128)S(1)} %add_multiply_fusion), channel_id=1, source_target_pairs={{0,32},{32,0},{64,96},{96,64},{128,160},{160,128},{192,224},{224,1... | collective-permute-start | bytes 98312 | tf_op jit(solution)/shard_map/ppermute | solution.py:30
  74.4 0.9 %collective-permute-done.4 = f32[16,512]{1,0:T(8,128)S(1)} collective-permute-done((f32[16,512]{1,0:T(8,128)S(1)}, f32[16,512]{1,0:T(8,128)S(1)}, u32[]{:S(2)}, u32[]{:S(2)}) %collective-permute-start.4) | collective-permute-done | bytes 32800 | tf_op jit(solution)/shard_map/ppermute | solution.py:30
  75.3 0.6 broadcast_select_fusion
  (3 shorter events, 0.0 us)
Async XLA Ops:
  0.6 2.8 %copy-start.4 = (s32[512]{0:T(512)S(1)}, s32[512]{0:T(512)}, u32[]{:S(2)}) copy-start(s32[512]{0:T(512)} %param.12) | copy-start | bytes 6148
  34.5 4.9 %collective-permute-start = (bf16[512,512]{1,0:T(8,128)(2,1)S(1)}, bf16[512,512]{1,0:T(8,128)(2,1)S(1)}, u32[]{:S(2)}, u32[]{:S(2)}) collective-permute-start(bf16[512,512]{1,0:T(8,128)(2,1)S(1)} %symmetric_matrix.1.matrix_ref), channel_id=1, source_target_pairs={{0,32},{32,0},{64,96},{96,64},{128,160},{160,128},{192,224},{224,1... | collective-permute-start | bytes 1572872 | tf_op jit(solution)/shard_map/ppermute | solution.py:30
  43.6 2.0 %collective-permute-start.1 = (bf16[512,512]{1,0:T(8,128)(2,1)S(1)}, bf16[512,512]{1,0:T(8,128)(2,1)S(1)}, u32[]{:S(2)}, u32[]{:S(2)}) collective-permute-start(bf16[512,512]{1,0:T(8,128)(2,1)S(1)} %get-tuple-element.95), channel_id=1, source_target_pairs={{0,32},{32,0},{64,96},{96,64},{128,160},{160,128},{192,224},{224,1... | collective-permute-start | bytes 1572872 | tf_op jit(solution)/shard_map/ppermute | solution.py:30
  59.9 4.7 %collective-permute-start.2 = (f32[16,512]{1,0:T(8,128)S(1)}, f32[16,512]{1,0:T(8,128)S(1)}, u32[]{:S(2)}, u32[]{:S(2)}) collective-permute-start(f32[16,512]{1,0:T(8,128)S(1)} %convert_reduce_fusion), channel_id=1, source_target_pairs={{0,64},{32,96},{64,0},{96,32},{128,192},{160,224},{192,128},{224,1... | collective-permute-start | bytes 98312 | tf_op jit(solution)/shard_map/ppermute | solution.py:30
  64.6 5.5 %collective-permute-start.3 = (f32[16,512]{1,0:T(8,128)S(1)}, f32[16,512]{1,0:T(8,128)S(1)}, u32[]{:S(2)}, u32[]{:S(2)}) collective-permute-start(f32[16,512]{1,0:T(8,128)S(1)} %add.18), channel_id=1, source_target_pairs={{0,192},{32,224},{64,128},{96,160},{128,64},{160,96},{192,0},{224,... | collective-permute-start | bytes 98312 | tf_op jit(solution)/shard_map/ppermute | solution.py:30
  70.1 5.2 %collective-permute-start.4 = (f32[16,512]{1,0:T(8,128)S(1)}, f32[16,512]{1,0:T(8,128)S(1)}, u32[]{:S(2)}, u32[]{:S(2)}) collective-permute-start(f32[16,512]{1,0:T(8,128)S(1)} %add_multiply_fusion), channel_id=1, source_target_pairs={{0,32},{32,0},{64,96},{96,64},{128,160},{160,128},{192,224},{224,1... | collective-permute-start | bytes 98312 | tf_op jit(solution)/shard_map/ppermute | solution.py:30
